TPU v7x, 32 devices: a whole 2x2x4 slice. The times are simulated.
32 devices in a mesh: seq: 8 (over z, x), head: 4 (over y, core).
Axes of the slice: x: 2, y: 2, z: 4, core: 2. Of those that a mesh axis runs over, the one named last changes fastest.
Arguments:
- query_rows: bfloat16 [16384, 1024], P('seq', 'head'), may hold values from -8 to 8
- key_rows: bfloat16 [16384, 1024], P('seq', 'head'), may hold values from -6 to 6
- value_rows: bfloat16 [16384, 1024], P('seq', 'head'), may hold values from -12 to 12
- out_grad: bfloat16 [16384, 1024], P('seq', 'head'), may hold values from -12 to 12
- block_perm: int32 [8, 64], P('head'), may hold values from 0 to 63, as said below
- cut_count: int32 [8], P('head'), may hold values from 1 to 4, as said below
- norm_gain: float32 [1024], P('head'), may hold values from 0.1 to 1.9
Outputs:
- normed_out: bfloat16 [16384, 1024], P('seq', 'head')
- query_grad: bfloat16 [16384, 1024], P('seq', 'head')
- key_grad: bfloat16 [16384, 1024], P('seq', 'head')
- value_grad: bfloat16 [16384, 1024], P('seq', 'head')
- gain_grad: float32 [1024], P('head')
Inputs may be any that keep to these rules, and one draw needn't show every extreme that they name: `block_perm`: each row is a permutation of 0 to 63. For every head, of the 8 blocks d * 8 to (d + 1) * 8 - 1, at most 1 are paired with blocks of one range s * 8 to (s + 1) * 8 - 1, and some pair (d, s) reaches 1. `cut_count`: some head has exactly 4.
All inputs are finite; a program needn't handle non-finite values.
Results may differ from a plain program's by a relative error of at most 0.0071.
Values may be sent and summed in bfloat16 or wider, within the bound.
A program may use at most 128 MiB of HBM per device.

v0:
```python
from functools import partial
import jax
import jax.numpy as jnp
from jax import lax
from jax.sharding import PartitionSpec as P

BLOCK = 256
KCUT = 4


def split_heads(rows, heads):
    tokens = rows.shape[0]
    width = rows.shape[1] // heads
    return rows.reshape(tokens // BLOCK, BLOCK, heads, width).transpose(2, 0, 1, 3)


def merge_heads(parts):
    return parts.transpose(1, 2, 0, 3).reshape(
        parts.shape[1] * parts.shape[2], parts.shape[0] * parts.shape[3]
    )


def to_slots(rows, slot_of, count):
    match = slot_of[:, None, :] == jnp.arange(count)[None, :, None]
    chosen = jnp.sum(jnp.where(match, jnp.arange(rows.shape[1])[None, None, :], 0), axis=2)
    filled = jnp.any(match, axis=2)
    picked = jax.vmap(lambda piece, which: piece[which])(rows, chosen)
    shape = filled.shape + (1,) * (rows.ndim - 2)
    return jnp.where(filled.reshape(shape), picked, jnp.zeros_like(picked))


def from_slots(slot_rows, slot_of):
    return jax.vmap(lambda piece, which: piece[which])(slot_rows, slot_of)


def attend(query, own_rows, paired_rows, cutoff_rows, live, scale):
    width = query.shape[-1]
    span = own_rows.shape[1]
    count = cutoff_rows.shape[0]
    own = jnp.einsum(
        "gqd,gkd->gqk", query, own_rows[..., :width], preferred_element_type=jnp.float32
    )
    pair = jnp.einsum(
        "gqd,gkd->gqk", query, paired_rows[..., :width], preferred_element_type=jnp.float32
    )
    cut = jnp.einsum(
        "gqd,ckd->gqck", query, cutoff_rows[..., :width], preferred_element_type=jnp.float32
    )
    cut = cut.reshape(query.shape[0], query.shape[1], count * span)
    scores = jnp.concatenate([own, pair, cut], axis=-1) * scale
    open_keys = jnp.concatenate([jnp.ones((2 * span,), jnp.bool_), jnp.repeat(live, span)])
    scores = jnp.where(open_keys, scores, -1e30)
    top = jnp.max(scores, axis=-1)
    weights = jnp.exp(scores - top[..., None])
    total = jnp.sum(weights, axis=-1)
    return (weights / total[..., None], top, total)


def forward_head(query, own_rows, paired_rows, cutoff_rows, live, scale):
    width = query.shape[-1]
    span = query.shape[1]
    groups = query.shape[0] // 2
    count = cutoff_rows.shape[0]

    def forward_step(pieces):
        query_part, own_part, pair_part = pieces
        prob, top, total = attend(query_part, own_part, pair_part, cutoff_rows, live, scale)
        weights = prob.astype(jnp.bfloat16)
        result = jnp.einsum(
            "gqk,gkd->gqd",
            weights[..., :span],
            own_part[..., width:],
            preferred_element_type=jnp.float32,
        )
        result = result + jnp.einsum(
            "gqk,gkd->gqd",
            weights[..., span : 2 * span],
            pair_part[..., width:],
            preferred_element_type=jnp.float32,
        )
        cut_weight = weights[..., 2 * span :].reshape(2, span, count, span)
        result = result + jnp.einsum(
            "gqck,ckd->gqd",
            cut_weight,
            cutoff_rows[..., width:],
            preferred_element_type=jnp.float32,
        )
        return result.astype(jnp.bfloat16)

    result = lax.map(
        forward_step,
        (
            query.reshape(groups, 2, span, width),
            own_rows.reshape(groups, 2, span, 2 * width),
            paired_rows.reshape(groups, 2, span, 2 * width),
        ),
    )
    return result.reshape(query.shape)


def backward_head(query, own_rows, paired_rows, cutoff_rows, live, cotangent, scale):
    width = query.shape[-1]
    span = query.shape[1]
    groups = query.shape[0] // 2
    count = cutoff_rows.shape[0]

    def backward_step(carry, pieces):
        query_part, own_part, pair_part, cot_part = pieces
        prob, top, total = attend(query_part, own_part, pair_part, cutoff_rows, live, scale)
        weights = prob.astype(jnp.bfloat16)
        dprob = jnp.concatenate(
            [
                jnp.einsum(
                    "gqd,gkd->gqk",
                    cot_part,
                    own_part[..., width:],
                    preferred_element_type=jnp.float32,
                ),
                jnp.einsum(
                    "gqd,gkd->gqk",
                    cot_part,
                    pair_part[..., width:],
                    preferred_element_type=jnp.float32,
                ),
                jnp.einsum(
                    "gqd,ckd->gqck",
                    cot_part,
                    cutoff_rows[..., width:],
                    preferred_element_type=jnp.float32,
                ).reshape(2, span, count * span),
            ],
            axis=-1,
        )
        delta = jnp.sum(prob * dprob, axis=-1)
        dscore = (prob * (dprob - delta[..., None]) * scale).astype(jnp.bfloat16)
        cut_score = dscore[..., 2 * span :].reshape(2, span, count, span)
        cut_weight = weights[..., 2 * span :].reshape(2, span, count, span)
        query_grad = jnp.einsum(
            "gqk,gkd->gqd",
            dscore[..., :span],
            own_part[..., :width],
            preferred_element_type=jnp.float32,
        )
        query_grad = query_grad + jnp.einsum(
            "gqk,gkd->gqd",
            dscore[..., span : 2 * span],
            pair_part[..., :width],
            preferred_element_type=jnp.float32,
        )
        query_grad = query_grad + jnp.einsum(
            "gqck,ckd->gqd", cut_score, cutoff_rows[..., :width], preferred_element_type=jnp.float32
        )
        own_grad = jnp.concatenate(
            [
                jnp.einsum(
                    "gqk,gqd->gkd",
                    dscore[..., :span],
                    query_part,
                    preferred_element_type=jnp.float32,
                ),
                jnp.einsum(
                    "gqk,gqd->gkd",
                    weights[..., :span],
                    cot_part,
                    preferred_element_type=jnp.float32,
                ),
            ],
            axis=-1,
        )
        pair_grad = jnp.concatenate(
            [
                jnp.einsum(
                    "gqk,gqd->gkd",
                    dscore[..., span : 2 * span],
                    query_part,
                    preferred_element_type=jnp.float32,
                ),
                jnp.einsum(
                    "gqk,gqd->gkd",
                    weights[..., span : 2 * span],
                    cot_part,
                    preferred_element_type=jnp.float32,
                ),
            ],
            axis=-1,
        )
        cut_grad = jnp.concatenate(
            [
                jnp.einsum(
                    "gqck,gqd->ckd", cut_score, query_part, preferred_element_type=jnp.float32
                ),
                jnp.einsum(
                    "gqck,gqd->ckd", cut_weight, cot_part, preferred_element_type=jnp.float32
                ),
            ],
            axis=-1,
        )
        return (
            carry + cut_grad,
            (query_grad.astype(jnp.bfloat16), own_grad, pair_grad, top, total, delta),
        )

    start = jnp.zeros((count, span, 2 * width), jnp.float32)
    cut_sum, outputs = lax.scan(
        backward_step,
        start,
        (
            query.reshape(groups, 2, span, width),
            own_rows.reshape(groups, 2, span, 2 * width),
            paired_rows.reshape(groups, 2, span, 2 * width),
            cotangent.reshape(groups, 2, span, width),
        ),
    )
    query_grad, own_grad, pair_grad, top, total, delta = outputs
    blocks = query.shape[0]
    return (
        query_grad.reshape(query.shape),
        own_grad.reshape(own_rows.shape),
        pair_grad.reshape(own_rows.shape),
        cut_sum,
        top.reshape(blocks, span),
        total.reshape(blocks, span),
        delta.reshape(blocks, span),
    )


def owner_pair(query, cotangent, top, total, delta, own_rows, scale):
    width = query.shape[-1]
    scores = (
        jnp.einsum("jqd,jkd->jqk", query, own_rows[..., :width], preferred_element_type=jnp.float32)
        * scale
    )
    prob = jnp.exp(scores - top[..., None]) / total[..., None]
    dprob = jnp.einsum(
        "jqd,jkd->jqk", cotangent, own_rows[..., width:], preferred_element_type=jnp.float32
    )
    dscore = (prob * (dprob - delta[..., None]) * scale).astype(jnp.bfloat16)
    return jnp.concatenate(
        [
            jnp.einsum("jqk,jqd->jkd", dscore, query, preferred_element_type=jnp.float32),
            jnp.einsum(
                "jqk,jqd->jkd",
                prob.astype(jnp.bfloat16),
                cotangent,
                preferred_element_type=jnp.float32,
            ),
        ],
        axis=-1,
    )


def body(query_rows, key_rows, value_rows, out_grad, block_perm, cut_count, norm_gain):
    heads = block_perm.shape[0]
    width = query_rows.shape[1] // heads
    blocks = query_rows.shape[0] // BLOCK
    seq_count = lax.axis_size("seq")
    head_count = lax.axis_size("head")
    capacity = (blocks + seq_count - 1) // seq_count
    slot_count = seq_count * capacity
    scale = width ** (-0.5)
    position = lax.axis_index("seq")
    query_h = split_heads(query_rows, heads)
    grad_h = split_heads(out_grad, heads)
    own_rows = jnp.concatenate(
        [split_heads(key_rows, heads), split_heads(value_rows, heads)], axis=-1
    )
    local_perm = lax.dynamic_slice_in_dim(block_perm, position * blocks, blocks, 1)
    source_dev = local_perm // blocks
    lower = jnp.arange(blocks)[:, None] > jnp.arange(blocks)[None, :]
    same_source = source_dev[:, :, None] == source_dev[:, None, :]
    recv_slot = source_dev * capacity + jnp.sum(same_source & lower[None], axis=2)
    owned = position * blocks + jnp.arange(blocks)
    hits = block_perm[:, None, :] == owned[None, :, None]
    dest_global = jnp.sum(
        jnp.where(hits, jnp.arange(block_perm.shape[1])[None, None, :], 0), axis=2
    )
    dest_dev = dest_global // blocks
    dest_local = dest_global % blocks
    before = (dest_dev[:, :, None] == dest_dev[:, None, :]) & (
        dest_local[:, None, :] < dest_local[:, :, None]
    )
    send_slot = dest_dev * capacity + jnp.sum(before, axis=2)
    own_send = to_slots(own_rows, send_slot, slot_count)
    query_send = to_slots(query_h, recv_slot, slot_count)
    own_recv, query_recv = (
        lax.all_to_all(own_send, "seq", split_axis=1, concat_axis=1, tiled=True),
        lax.all_to_all(query_send, "seq", split_axis=1, concat_axis=1, tiled=True),
    )
    query_owner = from_slots(query_recv, send_slot)
    paired_rows = from_slots(own_recv, recv_slot)
    cut_global = block_perm[:, :KCUT]
    cut_dev = cut_global // blocks
    cut_local = cut_global % blocks
    cut_pick = jax.vmap(lambda piece, which: piece[which])(own_rows, cut_local)
    cut_pick = jnp.where(
        (cut_dev == position)[:, :, None, None], cut_pick, jnp.zeros_like(cut_pick)
    )
    cutoff_rows = lax.psum(cut_pick.astype(jnp.float32).astype(jnp.bfloat16), "seq")
    live = jnp.arange(KCUT)[None, :] < cut_count[:, None]
    attn = jax.vmap(partial(forward_head, scale=scale))(
        query_h, own_rows, paired_rows, cutoff_rows, live
    )
    attn_f = attn.astype(jnp.float32)
    grad_f = grad_h.astype(jnp.float32)
    gain = norm_gain.reshape(heads, 1, 1, width)
    square_part = jnp.sum(attn_f * attn_f, axis=(0, 3))
    mix_part = jnp.sum(gain * grad_f * attn_f, axis=(0, 3))
    square_sum, mix_sum = lax.psum((square_part, mix_part), "head")
    features = head_count * heads * width
    scale_row = lax.rsqrt(square_sum / features + 1e-06)[None, :, :, None]
    normed = (attn_f * scale_row * gain).astype(jnp.bfloat16)
    gain_part = jnp.sum(grad_f * attn_f * scale_row, axis=(1, 2))
    cotangent = (
        scale_row * gain * grad_f - attn_f * scale_row**3 * mix_sum[None, :, :, None] / features
    ).astype(jnp.bfloat16)
    query_grad, own_grad, pair_grad, cut_grad, top, total, delta = jax.vmap(
        partial(backward_head, scale=scale)
    )(query_h, own_rows, paired_rows, cutoff_rows, live, cotangent)
    cot_send = to_slots(cotangent, recv_slot, slot_count)
    cot_recv = lax.all_to_all(cot_send, "seq", split_axis=1, concat_axis=1, tiled=True)
    top_send = to_slots(top, recv_slot, slot_count)
    total_send = to_slots(total, recv_slot, slot_count)
    delta_send = to_slots(delta, recv_slot, slot_count)
    top_recv, total_recv, delta_recv = (
        lax.all_to_all(top_send, "seq", split_axis=1, concat_axis=1, tiled=True),
        lax.all_to_all(total_send, "seq", split_axis=1, concat_axis=1, tiled=True),
        lax.all_to_all(delta_send, "seq", split_axis=1, concat_axis=1, tiled=True),
    )
    pair_full = jax.vmap(partial(owner_pair, scale=scale))(
        query_owner,
        from_slots(cot_recv, send_slot),
        from_slots(top_recv, send_slot),
        from_slots(total_recv, send_slot),
        from_slots(delta_recv, send_slot),
        own_rows,
    )
    pair_term = lax.optimization_barrier(pair_full.astype(jnp.bfloat16)).astype(jnp.float32)
    cut_total, gain_total = lax.psum((cut_grad, gain_part), "seq")
    match = (
        (cut_dev == position)[:, :, None]
        & (cut_local[:, :, None] == jnp.arange(blocks)[None, None, :])
    ).astype(jnp.float32)
    cut_term = jnp.einsum("hcj,hcqd->hjqd", match, cut_total, precision=lax.Precision.HIGHEST)
    total_grad = (own_grad + pair_term + cut_term).astype(jnp.bfloat16)
    return (
        merge_heads(normed),
        merge_heads(query_grad),
        merge_heads(total_grad[..., :width]),
        merge_heads(total_grad[..., width:]),
        gain_total.reshape(heads * width),
    )


def solution(mesh):
    placed = (
        P("seq", "head"),
        P("seq", "head"),
        P("seq", "head"),
        P("seq", "head"),
        P("head", None),
        P("head"),
        P("head"),
    )
    return jax.shard_map(
        body,
        mesh=mesh,
        in_specs=placed,
        out_specs=(
            P("seq", "head"),
            P("seq", "head"),
            P("seq", "head"),
            P("seq", "head"),
            P("head"),
        ),
        check_vma=False,
    )
```

profile of v0, /device:TPU:0, one launch (start us, length us, event | category | flops | bytes accessed | tf_op | source)
XLA Modules:
  0.0 683.0 jit_solution(10543006544791201384)
XLA Ops:
  15.9 3.1 copy_select_fusion
  19.0 7.3 %all-to-all-start = ((bf16[2,8,256,256]{3,2,0,1:T(8,128)(2,1)}), bf16[2,8,256,256]{3,2,0,1:T(8,128)(2,1)}, u32[]{:S(2)}, u32[]{:S(2)}) async-start(bf16[2,8,256,256]{3,2,0,1:T(8,128)(2,1)} %copy_select_fusion), calls=%async_computation | async-start | bytes 4194304 | tf_op jit(solution)/shard_map/all_to_all | solution.py:286
  36.0 51.3 %all-to-all-done = bf16[2,8,256,256]{3,2,0,1:T(8,128)(2,1)} async-done(((bf16[2,8,256,256]{3,2,0,1:T(8,128)(2,1)}), bf16[2,8,256,256]{3,2,0,1:T(8,128)(2,1)}, u32[]{:S(2)}, u32[]{:S(2)}) %all-to-all-start) | async-done | bytes 2097184 | tf_op jit(solution)/shard_map/all_to_all | solution.py:286
  91.1 3.1 copy.276
  94.2 40.7 %all-reduce.5.cloned.1.call-done = bf16[2,4,256,256]{3,2,1,0:T(8,128)(2,1)} async-done(((bf16[2,4,256,256]{3,2,1,0:T(8,128)(2,1)}), bf16[2,4,256,256]{3,2,1,0:T(8,128)(2,1)}) %all-reduce.5.cloned.1.call-update) | async-done | bytes 1048592 | tf_op jit(solution)/shard_map/psum | solution.py:298
  136.1 76.6 %while.32 = (s32[]{:T(128)}, bf16[4,2,2,256,128]{4,3,2,0,1:T(8,128)(2,1)}, bf16[4,2,2,256,128]{4,3,2,1,0:T(8,128)(2,1)S(1)}, bf16[4,2,2,256,256]{4,3,2,1,0:T(8,1...) while((s32[]{:T(128)}, ...), condition=%wide.region_9.10_spmd.clone, body=%wide.region_6.9_spmd.clone.sunk | while | flops 818284032 | bytes 55597728 | solution.py:90
  142.7 5.4 copy.414
  148.3 3.7 fusion.235
  161.8 5.4 copy.414
  167.4 3.7 fusion.235
  181.0 5.4 copy.414
  186.6 3.7 fusion.235
  200.1 5.4 copy.414
  205.7 3.7 fusion.235
  217.2 6.9 %psum.36 = f32[8,256]{1,0:T(8,128)S(1)} all-reduce(f32[8,256]{1,0:T(8,128)S(1)} %reduce_sum.131), channel_id=1, replica_groups=mesh['seq'=8,'head'=4] {'head'}, use_global_device_ids=true, to_apply=%region_11.12 | all-reduce | flops 2048 | bytes 16384 | tf_op jit(solution)/shard_map/psum | solution.py:308
  227.0 6.3 psum.37
  233.3 3.2 fusion.113
  237.7 237.2 %while.33 = (s32[]{:T(128)}, f32[2,4,256,256]{2,3,1,0:T(8,128)}, bf16[4,2,2,256,128]{4,3,2,0,1:T(8,128)(2,1)}, f32[4,2,2,256,256]{3,4,2,1,0:T(8,128)}, f32[4,2,2...) while((s32[]{:T(128)}, f32[2,4,256,256]{2,3,1,0:T(8,128)}, ...), condition=%wide.region_18.19_spmd.clone, body=%wide.region_14.18_spmd.clone.sunk | while | flops 1934750720 | bytes 244144336 | solution.py:204
  243.4 5.4 copy.417
  258.1 5.4 copy.416
  263.5 5.6 multiply_reduce_fusion.3
  302.2 5.4 copy.417
  316.8 5.4 copy.416
  322.2 5.6 multiply_reduce_fusion.3
  352.4 3.5 maximum_add_fusion.2
  361.7 5.4 copy.417
  376.3 5.4 copy.416
  381.7 5.6 multiply_reduce_fusion.3
  411.9 3.5 maximum_add_fusion.2
  421.1 5.4 copy.417
  435.8 5.4 copy.416
  441.2 5.6 multiply_reduce_fusion.3
  471.4 3.5 maximum_add_fusion.2
  477.6 9.9 %all_to_all.30 = f32[2,8,256]{2,0,1:T(2,128)S(1)} all-to-all(f32[2,8,256]{2,0,1:T(2,128)S(1)} %get-tuple-element.372), channel_id=1, replica_groups=mesh['seq'=8,'head'=4] {'seq'}, dimensions={1} | all-to-all | bytes 32768 | tf_op jit(solution)/shard_map/all_to_all | solution.py:325
  487.5 3.3 all-to-all-start.3
  492.8 2.9 gather_fusion.9
  497.3 4.3 all-to-all-start.5
  501.6 3.0 copy_select_fusion.2
  504.6 3.6 all-to-all-done.5
  508.2 26.6 %all_to_all.31 = bf16[2,8,256,128]{3,2,0,1:T(8,128)(2,1)} all-to-all(bf16[2,8,256,128]{3,2,0,1:T(8,128)(2,1)} %get-tuple-element.373), channel_id=1, replica_groups=mesh['seq'=8,'head'=4] {'seq'}, dimensions={1} | all-to-all | bytes 2097152 | tf_op jit(solution)/shard_map/all_to_all | solution.py:287
  534.8 3.7 all-to-all-start.4
  540.5 4.6 copy.287
  549.6 28.1 %psum.39 = f32[256]{0:T(256)} all-reduce(f32[256]{0:T(256)S(1)} %bitcast.413), channel_id=1, replica_groups=mesh['seq'=8,'head'=4] {'seq'}, use_global_device_ids=true, to_apply=%region_23.24 | all-reduce | flops 256 | bytes 2048 | tf_op jit(solution)/shard_map/psum | solution.py:338
  587.4 4.8 fusion.121
  593.5 63.7 %all-reduce.7.cloned.1.call-done = f32[2,4,256,256]{3,1,2,0:T(4,128)} async-done(((f32[2,4,256,256]{3,1,2,0:T(4,128)}), f32[2,4,256,256]{3,1,2,0:T(4,128)}) %all-reduce.7.cloned.1.call-update) | async-done | bytes 2097168 | tf_op jit(solution)/shard_map/psum | solution.py:338
  657.2 5.3 fusion.130
  662.5 5.3 copy.306
  667.8 4.4 add_convert_fusion
  (454 shorter events, 259.1 us)
Async XLA Ops:
  15.9 10.5 %copy-start.31 = (s32[2,64]{1,0:T(2,128)S(1)}, s32[2,64]{1,0:T(2,128)}, u32[]{:S(2)}) copy-start(s32[2,64]{1,0:T(2,128)} %param.15) | copy-start | bytes 1540
  19.0 68.4 %all-to-all-start = ((bf16[2,8,256,256]{3,2,0,1:T(8,128)(2,1)}), bf16[2,8,256,256]{3,2,0,1:T(8,128)(2,1)}, u32[]{:S(2)}, u32[]{:S(2)}) async-start(bf16[2,8,256,256]{3,2,0,1:T(8,128)(2,1)} %copy_select_fusion), calls=%async_computation | async-start | bytes 4194304 | tf_op jit(solution)/shard_map/all_to_all | solution.py:286
  26.3 108.6 %all-reduce.5.cloned.1.call-start = ((), (), s32[]{:S(2)}) async-start(), calls=%async_computation.6 | async-start | bytes 2097152 | tf_op jit(solution)/shard_map/psum | solution.py:298
  89.1 47.0 %copy-start.42 = (s32[2]{0:T(128)S(1)}, s32[2]{0:T(128)}, u32[]{:S(2)}) copy-start(s32[2]{0:T(128)} %param.16) | copy-start | bytes 28
  212.7 11.5 %copy-start.19 = (f32[8,256,2,128]{3,2,1,0:T(2,128)S(1)}, f32[8,256,2,128]{3,2,1,0:T(2,128)}, u32[]{:S(2)}) copy-start(f32[8,256,2,128]{3,2,1,0:T(2,128)} %reshape.418) | copy-start | bytes 6291460
  212.7 11.5 %copy-start.41 = (f32[256]{0:T(256)S(1)}, f32[256]{0:T(256)}, u32[]{:S(2)}) copy-start(f32[256]{0:T(256)} %param.17) | copy-start | bytes 3076
  237.7 237.3 %copy-start.28 = (s32[16]{0:T(128)S(1)}, s32[16]{0:T(128)}, u32[]{:S(2)}) copy-start(s32[16]{0:T(128)} %reshape.321) | copy-start | bytes 196
  237.7 239.1 %copy-start.39 = (pred[2,8]{0,1:T(8,128)(4,1)S(1)}, pred[2,8]{0,1:T(8,128)(4,1)}, u32[]{:S(2)}) copy-start(pred[2,8]{0,1:T(8,128)(4,1)} %copy.288) | copy-start | bytes 52
  237.7 5.7 copy-start.7
  263.5 5.6 copy-start.1
  263.5 6.2 copy-start.2
  263.5 6.4 copy-start.6
  280.8 5.7 copy-start.8
  282.9 5.5 copy-start.5
  296.5 5.7 copy-start.7
  322.2 5.6 copy-start.1
  322.2 6.2 copy-start.2
  322.2 6.4 copy-start.6
  331.1 4.0 copy-start.3
  331.1 4.0 copy-start.4
  339.6 5.7 copy-start.8
  341.7 5.5 copy-start.5
  356.0 5.7 copy-start.7
  381.7 5.6 copy-start.1
  381.7 6.2 copy-start.2
  381.7 6.4 copy-start.6
  399.0 5.7 copy-start.8
  401.1 5.5 copy-start.5
  415.4 5.7 copy-start.7
  441.2 5.6 copy-start.1
  441.2 6.2 copy-start.2
  441.2 6.4 copy-start.6
  450.0 4.0 copy-start.3
  450.1 4.0 copy-start.4
  458.5 5.7 copy-start.8
  460.6 5.5 copy-start.5
  487.5 9.8 %all-to-all-start.3 = ((f32[2,8,256]{2,0,1:T(2,128)}), f32[2,8,256]{2,0,1:T(2,128)S(1)}, u32[]{:S(2)}, u32[]{:S(2)}) async-start(f32[2,8,256]{2,0,1:T(2,128)} %get-tuple-element.371), calls=%async_computation.3 | async-start | bytes 32768 | tf_op jit(solution)/shard_map/all_to_all | solution.py:326
  497.3 10.9 %all-to-all-start.5 = ((f32[2,8,256]{2,0,1:T(2,128)}), f32[2,8,256]{2,0,1:T(2,128)S(1)}, u32[]{:S(2)}, u32[]{:S(2)}) async-start(f32[2,8,256]{2,0,1:T(2,128)} %get-tuple-element.370), calls=%async_computation.5 | async-start | bytes 32768 | tf_op jit(solution)/shard_map/all_to_all | solution.py:327
  501.6 36.9 %copy-start.17 = (f32[2,4,256,256]{2,3,1,0:T(8,128)S(1)}, f32[2,4,256,256]{2,3,1,0:T(8,128)}, u32[]{:S(2)}) copy-start(f32[2,4,256,256]{2,3,1,0:T(8,128)} %get-tuple-element.120) | copy-start | bytes 6291460
  534.8 5.7 copy-start.34
  534.8 5.7 copy-start.36
  534.8 46.5 %all-to-all-start.4 = ((bf16[2,8,256,128]{3,2,0,1:T(8,128)(2,1)}), bf16[2,8,256,128]{3,2,0,1:T(8,128)(2,1)S(1)}, u32[]{:S(2)}, u32[]{:S(2)}) async-start(bf16[2,8,256,128]{3,2,0,1:T(8,128)(2,1)} %get-tuple-element.374), calls=%async_computation.4 | async-start | bytes 2097152 | tf_op jit(solution)/shard_map/all_to_all | solution.py:320
  538.5 118.7 %all-reduce.7.cloned.1.call-start = ((), (), s32[]{:S(2)}) async-start(), calls=%async_computation.7 | async-start | bytes 4194304 | tf_op jit(solution)/shard_map/psum | solution.py:338
  540.5 4.7 copy-start.25
  545.2 4.4 copy-start.40
  545.2 34.3 %copy-start.24 = (bf16[2,8,256,128]{3,2,0,1:T(8,128)(2,1)S(1)}, bf16[2,8,256,128]{3,2,0,1:T(8,128)(2,1)}, u32[]{:S(2)}) copy-start(bf16[2,8,256,128]{3,2,0,1:T(8,128)(2,1)} %all_to_all.31) | copy-start | bytes 3145732
  592.1 65.1 %copy-start.32 = (s32[2,4]{1,0:T(2,128)S(1)}, s32[2,4]{1,0:T(2,128)}, u32[]{:S(2)}) copy-start(s32[2,4]{1,0:T(2,128)} %get-tuple-element.351) | copy-start | bytes 100
  592.1 65.1 %copy-start.38 = (pred[2,4]{1,0:T(4,128)(4,1)S(1)}, pred[2,4]{1,0:T(4,128)(4,1)}, u32[]{:S(2)}) copy-start(pred[2,4]{1,0:T(4,128)(4,1)} %copy-done.37) | copy-start | bytes 28
  (55 other events, 128.4 us)
Sparse Core Ops, SparseCore 0:
  31.2 103.6 all-reduce.4
  542.9 114.2 all-reduce.6
where the time goes:
time: 686 us; the launch traced here: 683 us
  local copies, waits for them, and re-layouts  173 us (25%)
  waiting for transfers between devices  161 us (23%)
  matrix products  123 us (18%)
  other arithmetic  114 us (17%)
  blocking collectives  77.8 us (11%)
  starting transfers between devices  18.7 us (3%)
  between operations  14.6 us (2%)
    psum x1, waiting for transfers between devices, body(): cut_total, gain_total = lax.psum((cut_grad, gain_part), 'seq')  63.7 us
    all_to_all x1, waiting for transfers between devices, body(): lax.all_to_all(own_send, 'seq', split_axis=1, concat_axis=1, tiled=True)  51.3 us
    reshape x8, local copies, waits for them, and re-layouts, attend(): cut = cut.reshape(query.shape[0], query.shape[1], count * span)  43.2 us
    psum x1, waiting for transfers between devices, body(): lax.psum(cut_pick.astype(jnp.float32).astype(jnp.bfloat16), 'seq')  40.7 us
    psum x1, blocking collectives, body(): cut_total, gain_total = lax.psum((cut_grad, gain_part), 'seq')  28.1 us
    all_to_all x1, blocking collectives, body(): lax.all_to_all(query_send, 'seq', split_axis=1, concat_axis=1, tiled=True)  26.6 us
    reduce_sum x4, other arithmetic, backward_step(): delta = jnp.sum(prob * dprob, axis=-1)  22.4 us
    reshape x4, local copies, waits for them, and re-layouts, backward_step(): dprob = jnp.concatenate([jnp.einsum('gqd,gkd->gqk', cot_part, own_part[.....  21.7 us
  transfers between devices with their start and end apart: 6, of which 5 were waited for; matrix products, arithmetic and copies ran while one was open for 7% of the time, Pallas kernels for 0%

commit v1 on v0

--- a/solution.py
+++ b/solution.py
@@ -6,6 +6,10 @@
 
 BLOCK = 256
 KCUT = 4
+
+
+def change_pools(xs, lane_axis):
+    return lax.all_gather(xs, axis_name=lane_axis).sum(axis=0)
 
 
 def split_heads(rows, heads):
@@ -295,7 +299,7 @@
     cut_pick = jnp.where(
         (cut_dev == position)[:, :, None, None], cut_pick, jnp.zeros_like(cut_pick)
     )
-    cutoff_rows = lax.psum(cut_pick.astype(jnp.float32).astype(jnp.bfloat16), "seq")
+    cutoff_rows = change_pools(cut_pick.astype(jnp.float32).astype(jnp.bfloat16), lane_axis="seq")
     live = jnp.arange(KCUT)[None, :] < cut_count[:, None]
     attn = jax.vmap(partial(forward_head, scale=scale))(
         query_h, own_rows, paired_rows, cutoff_rows, live

time: 686 us -> 747 us (1.089)
  waiting for transfers between devices: 161 us -> 202 us
  matrix products: 123 us -> 135 us
    all_gather x0 -> x1, waiting for transfers between devices: none -> 61.6 us  [change_pools(): return lax.all_gather(xs, axis_name=lane_axis).sum(axis=0)]
    psum x1 -> x0, waiting for transfers between devices: 40.7 us -> none  [body(): lax.psum(cut_pick.astype(jnp.float32).astype(jnp.bfloat16), 'seq')]
    all_to_all x1, waiting for transfers between devices: 51.3 us -> 72.2 us  [body(): lax.all_to_all(own_send, 'seq', split_axis=1, concat_axis=1, tiled=True)]
    unnamed x61 -> x57, local copies, waits for them, and re-layouts: 17 us -> 16.4 us
where the time goes in v1:
time: 747 us; the launch traced here: 744 us
  waiting for transfers between devices  202 us (27%)
  local copies, waits for them, and re-layouts  179 us (24%)
  matrix products  135 us (18%)
  other arithmetic  117 us (16%)
  blocking collectives  77.7 us (10%)
  starting transfers between devices  18.7 us (3%)
  between operations  14.6 us (2%)
    all_to_all x1, waiting for transfers between devices, body(): lax.all_to_all(own_send, 'seq', split_axis=1, concat_axis=1, tiled=True)  72.2 us
    psum x1, waiting for transfers between devices, body(): cut_total, gain_total = lax.psum((cut_grad, gain_part), 'seq')  62.5 us
    all_gather x1, waiting for transfers between devices, change_pools(): return lax.all_gather(xs, axis_name=lane_axis).sum(axis=0)  61.6 us
    reshape x8, local copies, waits for them, and re-layouts, attend(): cut = cut.reshape(query.shape[0], query.shape[1], count * span)  43.3 us
    psum x1, blocking collectives, body(): cut_total, gain_total = lax.psum((cut_grad, gain_part), 'seq')  28.7 us
    all_to_all x1, blocking collectives, body(): lax.all_to_all(query_send, 'seq', split_axis=1, concat_axis=1, tiled=True)  26.8 us
    dot_general x8, matrix products, attend(): jnp.einsum('gqd,ckd->gqck', query, cutoff_rows[..., :width], preferred_el...  25.2 us
    reshape x4, local copies, waits for them, and re-layouts, backward_step(): dprob = jnp.concatenate([jnp.einsum('gqd,gkd->gqk', cot_part, own_part[.....  21.6 us
  transfers between devices with their start and end apart: 6, of which 5 were waited for; matrix products, arithmetic and copies ran while one was open for 7% of the time, Pallas kernels for 0%

profile of v1, /device:TPU:0, one launch (start us, length us, event | category | flops | bytes accessed | tf_op | source)
XLA Modules:
  0.0 743.7 jit_solution(10740071549612117477)
XLA Ops:
  20.3 7.3 all-to-all-start
  35.9 72.2 %all-to-all-done = bf16[2,8,256,256]{3,2,0,1:T(8,128)(2,1)} async-done(((bf16[2,8,256,256]{3,2,0,1:T(8,128)(2,1)}), bf16[2,8,256,256]{3,2,0,1:T(8,128)(2,1)}, u32[]{:S(2)}, u32[]{:S(2)}) %all-to-all-start) | async-done | bytes 2097184 | tf_op jit(solution)/shard_map/all_to_all | solution.py:290
  117.8 61.6 %all-gather.2.cloned.1.call-done = bf16[8,2,4,256,256]{4,3,2,1,0:T(8,128)(2,1)} async-done(((bf16[1,2,4,256,256]{4,3,2,1,0:T(8,128)(2,1)}), bf16[8,2,4,256,256]{4,3,2,1,0:T(8,128)(2,1)}) %all-gather.2.cloned.1.call-update) | async-done | bytes 8388624 | tf_op jit(solution)/shard_map/all_gather | solution.py:12
  179.4 5.0 reduce_sum.142
  185.6 76.1 %while.32 = (s32[]{:T(128)}, bf16[4,2,2,256,128]{4,3,2,0,1:T(8,128)(2,1)}, bf16[4,2,2,256,128]{4,3,2,1,0:T(8,128)(2,1)S(1)}, bf16[4,2,2,256,256]{4,3,2,1,0:T(8,1...) while((s32[]{:T(128)}, ...), condition=%wide.region_9.10_spmd.clone, body=%wide.region_6.9_spmd.clone.sunk | while | flops 818284032 | bytes 51403396 | solution.py:94
  192.1 5.4 copy.414
  197.7 3.7 fusion.235
  211.1 5.4 copy.414
  216.7 3.7 fusion.235
  230.2 5.4 copy.414
  235.7 3.7 fusion.235
  249.2 5.4 copy.414
  254.8 3.7 fusion.235
  266.1 5.9 psum.28
  275.5 6.6 psum.29
  282.2 3.7 fusion.113
  287.0 249.2 %while.33 = (s32[]{:T(128)}, f32[2,4,256,256]{2,3,1,0:T(8,128)}, bf16[4,2,2,256,128]{4,3,2,0,1:T(8,128)(2,1)}, f32[4,2,2,256,256]{3,4,2,1,0:T(8,128)}, f32[4,2,2...) while((s32[]{:T(128)}, f32[2,4,256,256]{2,3,1,0:T(8,128)}, ...), condition=%wide.region_18.19_spmd.clone, body=%wide.region_14.18_spmd.clone.sunk | while | flops 1934750720 | bytes 244146352 | solution.py:208
  291.1 3.6 fusion.268
  294.7 5.4 copy.417
  306.8 3.7 fusion.265
  310.4 5.4 copy.416
  315.8 5.1 multiply_reduce_fusion.3
  356.6 5.4 copy.417
  368.6 3.7 fusion.265
  372.3 5.4 copy.416
  377.7 5.1 multiply_reduce_fusion.3
  415.4 3.6 fusion.268
  419.0 5.4 copy.417
  431.0 3.7 fusion.265
  434.7 5.4 copy.416
  440.1 5.1 multiply_reduce_fusion.3
  477.8 3.6 fusion.268
  481.4 5.4 copy.417
  493.5 3.7 fusion.265
  497.1 5.4 copy.416
  502.5 5.1 multiply_reduce_fusion.3
  538.8 9.6 %all_to_all.30 = f32[2,8,256]{2,0,1:T(2,128)S(1)} all-to-all(f32[2,8,256]{2,0,1:T(2,128)S(1)} %get-tuple-element.372), channel_id=1, replica_groups=mesh['seq'=8,'head'=4] {'seq'}, dimensions={1} | all-to-all | bytes 32768 | tf_op jit(solution)/shard_map/all_to_all | solution.py:329
  558.3 4.3 all-to-all-start.5
  565.4 3.7 all-to-all-done.5
  569.1 26.8 %all_to_all.31 = bf16[2,8,256,128]{3,2,0,1:T(8,128)(2,1)} all-to-all(bf16[2,8,256,128]{3,2,0,1:T(8,128)(2,1)} %get-tuple-element.373), channel_id=1, replica_groups=mesh['seq'=8,'head'=4] {'seq'}, dimensions={1} | all-to-all | bytes 2097152 | tf_op jit(solution)/shard_map/all_to_all | solution.py:291
  595.9 3.7 all-to-all-start.4
  601.7 4.6 copy.286
  610.7 28.7 %psum.31 = f32[256]{0:T(256)} all-reduce(f32[256]{0:T(256)S(1)} %bitcast.413), channel_id=1, replica_groups=mesh['seq'=8,'head'=4] {'seq'}, use_global_device_ids=true, to_apply=%region_23.24 | all-reduce | flops 256 | bytes 2048 | tf_op jit(solution)/shard_map/psum | solution.py:342
  649.2 4.8 fusion.121
  655.4 62.5 %all-reduce.4.cloned.1.call-done = f32[2,4,256,256]{3,1,2,0:T(4,128)} async-done(((f32[2,4,256,256]{3,1,2,0:T(4,128)}), f32[2,4,256,256]{3,1,2,0:T(4,128)}) %all-reduce.4.cloned.1.call-update) | async-done | bytes 2097168 | tf_op jit(solution)/shard_map/psum | solution.py:342
  717.9 5.3 fusion.130
  723.3 5.3 copy.305
  728.5 4.4 add_convert_fusion
  (443 shorter events, 276.2 us)
Async XLA Ops:
  7.2 172.3 %all-gather.2.cloned.1.call-start = ((), (), s32[]{:S(2)}) async-start(), calls=%async_computation.6 | async-start | bytes 9437184 | tf_op jit(solution)/shard_map/all_gather | solution.py:12
  14.6 5.7 copy-start.30
  20.3 87.8 %all-to-all-start = ((bf16[2,8,256,256]{3,2,0,1:T(8,128)(2,1)}), bf16[2,8,256,256]{3,2,0,1:T(8,128)(2,1)}, u32[]{:S(2)}, u32[]{:S(2)}) async-start(bf16[2,8,256,256]{3,2,0,1:T(8,128)(2,1)} %copy_select_fusion), calls=%async_computation | async-start | bytes 4194304 | tf_op jit(solution)/shard_map/all_to_all | solution.py:290
  117.8 67.8 %copy-start.39 = (s32[2]{0:T(128)S(1)}, s32[2]{0:T(128)}, u32[]{:S(2)}) copy-start(s32[2]{0:T(128)} %param.16) | copy-start | bytes 28
  261.7 10.3 %copy-start.38 = (f32[256]{0:T(256)S(1)}, f32[256]{0:T(256)}, u32[]{:S(2)}) copy-start(f32[256]{0:T(256)} %param.17) | copy-start | bytes 3076
  287.0 249.2 %copy-start.26 = (s32[16]{0:T(128)S(1)}, s32[16]{0:T(128)}, u32[]{:S(2)}) copy-start(s32[16]{0:T(128)} %reshape.328) | copy-start | bytes 196
  287.0 251.1 %copy-start.36 = (pred[2,8]{0,1:T(8,128)(4,1)S(1)}, pred[2,8]{0,1:T(8,128)(4,1)}, u32[]{:S(2)}) copy-start(pred[2,8]{0,1:T(8,128)(4,1)} %copy.287) | copy-start | bytes 52
  287.0 7.7 %copy-start.7 = (bf16[2,4,256,256]{3,2,1,0:T(8,128)(2,1)}, bf16[2,4,256,256]{3,2,1,0:T(8,128)(2,1)S(1)}, u32[]{:S(2)}) copy-start(bf16[2,4,256,256]{3,2,1,0:T(8,128)(2,1)S(1)} %get-tuple-element.586) | copy-start | bytes 3145732 | tf_op jit(solution)/shard_map/vmap()/while
  315.8 5.1 copy-start.1
  315.8 6.2 copy-start.2
  315.8 6.4 copy-start.6
  324.7 4.0 copy-start.3
  328.7 4.5 copy-start.8
  334.2 6.4 copy-start.5
  343.5 5.4 copy-start.10
  348.9 7.7 %copy-start.7 = (bf16[2,4,256,256]{3,2,1,0:T(8,128)(2,1)}, bf16[2,4,256,256]{3,2,1,0:T(8,128)(2,1)S(1)}, u32[]{:S(2)}) copy-start(bf16[2,4,256,256]{3,2,1,0:T(8,128)(2,1)S(1)} %get-tuple-element.586) | copy-start | bytes 3145732 | tf_op jit(solution)/shard_map/vmap()/while
  377.7 5.1 copy-start.1
  377.7 6.2 copy-start.2
  377.7 6.4 copy-start.6
  390.5 4.5 copy-start.8
  395.9 6.4 copy-start.5
  405.2 6.1 copy-start.10
  411.3 7.7 %copy-start.7 = (bf16[2,4,256,256]{3,2,1,0:T(8,128)(2,1)}, bf16[2,4,256,256]{3,2,1,0:T(8,128)(2,1)S(1)}, u32[]{:S(2)}) copy-start(bf16[2,4,256,256]{3,2,1,0:T(8,128)(2,1)S(1)} %get-tuple-element.586) | copy-start | bytes 3145732 | tf_op jit(solution)/shard_map/vmap()/while
  440.1 5.1 copy-start.1
  440.1 6.2 copy-start.2
  440.1 6.4 copy-start.6
  452.9 4.5 copy-start.8
  458.4 6.4 copy-start.5
  467.6 6.1 copy-start.10
  473.7 7.7 %copy-start.7 = (bf16[2,4,256,256]{3,2,1,0:T(8,128)(2,1)}, bf16[2,4,256,256]{3,2,1,0:T(8,128)(2,1)S(1)}, u32[]{:S(2)}) copy-start(bf16[2,4,256,256]{3,2,1,0:T(8,128)(2,1)S(1)} %get-tuple-element.586) | copy-start | bytes 3145732 | tf_op jit(solution)/shard_map/vmap()/while
  502.5 5.1 copy-start.1
  502.5 6.2 copy-start.2
  502.5 6.4 copy-start.6
  515.4 4.5 copy-start.8
  520.8 6.4 copy-start.5
  530.1 6.1 copy-start.10
  548.4 9.8 %all-to-all-start.3 = ((f32[2,8,256]{2,0,1:T(2,128)}), f32[2,8,256]{2,0,1:T(2,128)S(1)}, u32[]{:S(2)}, u32[]{:S(2)}) async-start(f32[2,8,256]{2,0,1:T(2,128)} %get-tuple-element.371), calls=%async_computation.3 | async-start | bytes 32768 | tf_op jit(solution)/shard_map/all_to_all | solution.py:330
  558.3 10.9 %all-to-all-start.5 = ((f32[2,8,256]{2,0,1:T(2,128)}), f32[2,8,256]{2,0,1:T(2,128)S(1)}, u32[]{:S(2)}, u32[]{:S(2)}) async-start(f32[2,8,256]{2,0,1:T(2,128)} %get-tuple-element.370), calls=%async_computation.5 | async-start | bytes 32768 | tf_op jit(solution)/shard_map/all_to_all | solution.py:331
  562.5 37.2 %copy-start.16 = (f32[2,4,256,256]{2,3,1,0:T(8,128)S(1)}, f32[2,4,256,256]{2,3,1,0:T(8,128)}, u32[]{:S(2)}) copy-start(f32[2,4,256,256]{2,3,1,0:T(8,128)} %get-tuple-element.120) | copy-start | bytes 6291460
  595.9 5.6 copy-start.31
  595.9 5.6 copy-start.33
  595.9 47.1 %all-to-all-start.4 = ((bf16[2,8,256,128]{3,2,0,1:T(8,128)(2,1)}), bf16[2,8,256,128]{3,2,0,1:T(8,128)(2,1)S(1)}, u32[]{:S(2)}, u32[]{:S(2)}) async-start(bf16[2,8,256,128]{3,2,0,1:T(8,128)(2,1)} %get-tuple-element.374), calls=%async_computation.4 | async-start | bytes 2097152 | tf_op jit(solution)/shard_map/all_to_all | solution.py:324
  599.7 118.3 %all-reduce.4.cloned.1.call-start = ((), (), s32[]{:S(2)}) async-start(), calls=%async_computation.7 | async-start | bytes 4194304 | tf_op jit(solution)/shard_map/psum | solution.py:342
  601.7 4.6 copy-start.23
  606.3 4.4 copy-start.37
  606.3 35.0 %copy-start.22 = (bf16[2,8,256,128]{3,2,0,1:T(8,128)(2,1)S(1)}, bf16[2,8,256,128]{3,2,0,1:T(8,128)(2,1)}, u32[]{:S(2)}) copy-start(bf16[2,8,256,128]{3,2,0,1:T(8,128)(2,1)} %all_to_all.31) | copy-start | bytes 3145732
  654.0 63.9 %copy-start.29 = (s32[2,4]{1,0:T(2,128)S(1)}, s32[2,4]{1,0:T(2,128)}, u32[]{:S(2)}) copy-start(s32[2,4]{1,0:T(2,128)} %get-tuple-element.351) | copy-start | bytes 100
  654.0 63.9 %copy-start.35 = (pred[2,4]{1,0:T(4,128)(4,1)S(1)}, pred[2,4]{1,0:T(4,128)(4,1)}, u32[]{:S(2)}) copy-start(pred[2,4]{1,0:T(4,128)(4,1)} %copy-done.34) | copy-start | bytes 28
  (49 other events, 111.7 us)
Sparse Core Ops, SparseCore 0:
  13.7 165.6 all-gather.1
  604.1 113.7 all-reduce.3
